TPU v7x, 512 devices: a whole 4x8x8 slice. The times are simulated.
512 devices in a mesh: section: 4 (over x), seq: 8 (over y), dp: 16 (over z, core).
Axes of the slice: x: 4, y: 8, z: 8, core: 2. Of those that a mesh axis runs over, the one named last changes fastest.
Arguments:
- queries: bfloat16 [16, 1024, 32, 128], P('dp', 'seq', 'section'), may hold values from -18 to 18
- video_keys: bfloat16 [16, 1024, 32, 128], P('dp', 'seq', 'section'), may hold values from -18 to 18
- video_values: bfloat16 [16, 1024, 32, 128], P('dp', 'seq', 'section'), may hold values from -6 to 6
- cross_queries: bfloat16 [16, 1024, 32, 128], P('dp', 'seq', 'section'), may hold values from -8 to 8
- self_cotangent: bfloat16 [16, 1024, 32, 128], P('dp', 'seq', 'section'), may hold values from -6 to 6
- cross_cotangent: bfloat16 [16, 1024, 32, 128], P('dp', 'seq', 'section'), may hold values from -6 to 6
- caption_states: bfloat16 [16, 512, 4096], P('dp', 'seq'), may hold values from -400 to 400
- caption_gain: float32 [4096], replicated, may hold values from 0.25 to 1.75
- key_weight: bfloat16 [4096, 4096], P('dp', ('section', 'seq')), may hold values from -0.09375 to 0.09375
- value_weight: bfloat16 [4096, 4096], P('dp', ('section', 'seq')), may hold values from -0.09375 to 0.09375
- video_length: int32 [16], replicated, may hold values from 512 to 1024, as said below
- caption_length: int32 [16], replicated, may hold values from 128 to 512, as said below
Outputs:
- query_gradient: bfloat16 [16, 1024, 32, 128], P('dp', 'seq', 'section')
- key_gradient: bfloat16 [16, 1024, 32, 128], P('dp', 'seq', 'section')
- value_gradient: bfloat16 [16, 1024, 32, 128], P('dp', 'seq', 'section')
- cross_query_gradient: bfloat16 [16, 1024, 32, 128], P('dp', 'seq', 'section')
- key_weight_gradient: float32 [4096, 4096], P('dp', ('section', 'seq'))
- value_weight_gradient: float32 [4096, 4096], P('dp', ('section', 'seq'))
Inputs may be any that keep to these rules, and one draw needn't show every extreme that they name: `video_length`: some clip has all 1024 tokens valid. `caption_length`: some clip has all 512 caption tokens valid.
All inputs are finite; a program needn't handle non-finite values.
Results may differ from a plain program's by a relative error of at most 0.018.
Values may be sent and summed in bfloat16 or wider, within the bound.
A program may use at most 64 MiB of HBM per device.

v0:
```python
import math
import jax
import jax.numpy as jnp
from jax import lax
from jax.sharding import PartitionSpec as P

norm_epsilon = 1e-06


def sent_together(arrays, axis, dim, along):
    ends, at = ([], 0)
    for a in arrays[:-1]:
        at += a.shape[along]
        ends.append(at)
    both = jnp.concatenate(arrays, axis=along)
    return tuple(jnp.split(lax.all_gather(both, axis, axis=dim, tiled=True), ends, axis=along))


def side_by_side(arrays, axis, split_dim, concat_dim, along):
    widths = [a.shape[along] for a in arrays]
    both = jnp.concatenate(arrays, axis=along)
    out = lax.all_to_all(both, axis, split_axis=split_dim, concat_axis=concat_dim, tiled=True)
    return tuple(jnp.split(out, [sum(widths[:k]) for k in range(1, len(widths))], axis=along))


def normalize_rows(states, caption_gain):
    values = states.astype(jnp.float32)
    mean_square = jnp.mean(values * values, axis=-1, keepdims=True)
    return (values * lax.rsqrt(mean_square + norm_epsilon) * caption_gain).astype(jnp.bfloat16)


def block_gradients(query_rows, cotangent_rows, key_rows, value_rows, key_limit, score_scale):
    scores = (
        jnp.einsum("qhd,khd->hqk", query_rows, key_rows, preferred_element_type=jnp.float32)
        * score_scale
    )
    columns = lax.broadcasted_iota(jnp.int32, scores.shape, 2)
    scores = jnp.where(columns < key_limit, scores, -jnp.inf)
    maxima = jnp.max(scores, axis=-1, keepdims=True)
    powers = jnp.exp(scores - maxima)
    weights = powers / jnp.sum(powers, axis=-1, keepdims=True)
    weights_low = weights.astype(jnp.bfloat16)
    weight_grad = jnp.einsum(
        "qhd,khd->hqk", cotangent_rows, value_rows, preferred_element_type=jnp.float32
    )
    row_total = jnp.sum(weights * weight_grad, axis=-1, keepdims=True)
    score_grad = (weights * (weight_grad - row_total) * score_scale).astype(jnp.bfloat16)
    query_grad = jnp.einsum(
        "hqk,khd->qhd", score_grad, key_rows, preferred_element_type=jnp.float32
    )
    key_grad = jnp.einsum(
        "hqk,qhd->khd", score_grad, query_rows, preferred_element_type=jnp.float32
    )
    value_grad = jnp.einsum(
        "hqk,qhd->khd", weights_low, cotangent_rows, preferred_element_type=jnp.float32
    )
    return (query_grad, key_grad, value_grad)


def attention_gradients(query_set, cotangent_set, key_set, value_set, key_limit, score_scale):
    row_count = query_set.shape[0]
    block_rows = math.gcd(row_count, 512)
    block_count = row_count // block_rows
    query_blocks = query_set.reshape((block_count, block_rows) + query_set.shape[1:])
    cotangent_blocks = cotangent_set.reshape((block_count, block_rows) + cotangent_set.shape[1:])

    def advance(totals, inputs):
        query_grad, key_grad, value_grad = block_gradients(
            inputs[0], inputs[1], key_set, value_set, key_limit, score_scale
        )
        return ((totals[0] + key_grad, totals[1] + value_grad), query_grad)

    empty = jnp.zeros(key_set.shape, jnp.float32)
    totals, query_grads = lax.scan(advance, (empty, empty), (query_blocks, cotangent_blocks))
    return (query_grads.reshape(query_set.shape), totals[0], totals[1])


def local(
    queries,
    video_keys,
    video_values,
    cross_queries,
    self_cotangent,
    cross_cotangent,
    caption_states,
    caption_gain,
    key_weight,
    value_weight,
    video_length,
    caption_length,
):
    head_size = queries.shape[3]
    score_scale = 1.0 / math.sqrt(head_size)
    head_width = key_weight.shape[1]
    local_heads = head_width // head_size
    normed = normalize_rows(lax.all_gather(caption_states, "seq", axis=1, tiled=True), caption_gain)
    normed_text = normed[0]
    caption_rows = normed_text.shape[0]
    pieces = sent_together((key_weight, value_weight), "dp", 0, 1)
    columns = normed_text
    text_keys = jnp.dot(columns, pieces[0], preferred_element_type=jnp.float32)
    text_values = jnp.dot(columns, pieces[1], preferred_element_type=jnp.float32)
    text_keys = text_keys.astype(jnp.bfloat16).reshape(caption_rows, local_heads, head_size)
    text_values = text_values.astype(jnp.bfloat16).reshape(caption_rows, local_heads, head_size)
    gathered = side_by_side(
        (queries, video_keys, video_values, cross_queries, self_cotangent, cross_cotangent),
        "seq",
        2,
        1,
        0,
    )
    head_queries, head_keys, head_values, head_cross, self_rows, cross_rows = (
        tensor[0] for tensor in gathered
    )
    clip_index = lax.axis_index("dp")
    video_limit = lax.dynamic_index_in_dim(video_length, clip_index, 0, keepdims=False)
    caption_limit = lax.dynamic_index_in_dim(caption_length, clip_index, 0, keepdims=False)
    positions = lax.broadcasted_iota(jnp.int32, (head_queries.shape[0], 1, 1), 0)
    nothing = jnp.zeros((), jnp.bfloat16)
    self_rows = jnp.where(positions < video_limit, self_rows, nothing)
    cross_rows = jnp.where(positions < video_limit, cross_rows, nothing)
    query_grad, key_grad, value_grad = attention_gradients(
        head_queries, self_rows, head_keys, head_values, video_limit, score_scale
    )
    cross_grad, text_key_grad, text_value_grad = attention_gradients(
        head_cross, cross_rows, text_keys, text_values, caption_limit, score_scale
    )
    returned = side_by_side(
        (
            query_grad.astype(jnp.bfloat16)[None],
            key_grad.astype(jnp.bfloat16)[None],
            value_grad.astype(jnp.bfloat16)[None],
            cross_grad.astype(jnp.bfloat16)[None],
        ),
        "seq",
        1,
        2,
        0,
    )
    key_cot = text_key_grad.astype(jnp.bfloat16).reshape(caption_rows, head_width)
    value_cot = text_value_grad.astype(jnp.bfloat16).reshape(caption_rows, head_width)
    stacked = jnp.concatenate((key_cot, value_cot), axis=1)
    contract_rows = (((0,), (0,)), ((), ()))
    columns = normed_text
    gradients = lax.psum_scatter(
        lax.dot_general(columns, stacked, contract_rows, preferred_element_type=jnp.float32).astype(
            jnp.bfloat16
        ),
        "dp",
        scatter_dimension=0,
        tiled=True,
    ).astype(jnp.float32)
    return (
        returned[0],
        returned[1],
        returned[2],
        returned[3],
        gradients[:, :head_width],
        gradients[:, head_width:],
    )


def solution(mesh):
    placed = (
        P("dp", "seq", "section", None),
        P("dp", "seq", "section", None),
        P("dp", "seq", "section", None),
        P("dp", "seq", "section", None),
        P("dp", "seq", "section", None),
        P("dp", "seq", "section", None),
        P("dp", "seq", None),
        P(),
        P("dp", ("section", "seq")),
        P("dp", ("section", "seq")),
        P(),
        P(),
    )
    return jax.shard_map(
        local,
        mesh=mesh,
        in_specs=placed,
        out_specs=(
            P("dp", "seq", "section", None),
            P("dp", "seq", "section", None),
            P("dp", "seq", "section", None),
            P("dp", "seq", "section", None),
            P("dp", ("section", "seq")),
            P("dp", ("section", "seq")),
        ),
        check_vma=False,
    )
```

profile of v0, /device:TPU:12, one launch (start us, length us, event | category | flops | bytes accessed | tf_op | source)
XLA Modules:
  0.0 239.1 jit_solution(1283080764883097908)
XLA Ops:
  8.0 1.5 pad_maximum_fusion.1
  9.6 1.7 copy_dynamic-update-slice_fusion.5
  11.3 1.7 copy_dynamic-update-slice_fusion.4
  13.8 0.8 copy_dynamic-update-slice_fusion.2
  14.5 0.8 copy_dynamic-update-slice_fusion.1
  16.1 7.5 %all-to-all-start = ((bf16[6,128,8,128]{3,1,0,2:T(8,128)(2,1)}), bf16[6,128,8,128]{3,1,0,2:T(8,128)(2,1)S(1)}, u32[]{:S(2)}, u32[]{:S(2)}) async-start(bf16[6,128,8,128]{3,1,0,2:T(8,128)(2,1)} %copy_dynamic-update-slice_fusion), calls=%async_computation | async-start | bytes 3145728 | tf_op jit(solution)/shard_map/all_to_all | solution.py:22
  25.5 50.6 %all-to-all-done = bf16[6,128,8,128]{3,1,0,2:T(8,128)(2,1)S(1)} async-done(((bf16[6,128,8,128]{3,1,0,2:T(8,128)(2,1)}), bf16[6,128,8,128]{3,1,0,2:T(8,128)(2,1)S(1)}, u32[]{:S(2)}, u32[]{:S(2)}) %all-to-all-start) | async-done | bytes 1572896 | tf_op jit(solution)/shard_map/all_to_all | solution.py:22
  76.2 0.8 fusion.65
  77.1 0.9 select_bitcast_fusion.1
  78.0 21.0 %all-gather.3.cloned.1.call-done = bf16[1,512,4096]{2,1,0:T(8,128)(2,1)} async-done(((bf16[1,64,4096]{2,1,0:T(8,128)(2,1)}), bf16[1,512,4096]{2,1,0:T(8,128)(2,1)}) %all-gather.3.cloned.1.call-update) | async-done | bytes 4194320 | tf_op jit(solution)/shard_map/all_gather | solution.py:96
  99.0 3.1 %fusion.49 = f32[512]{0:T(512)S(1)} fusion(bf16[1,512,4096]{2,1,0:T(8,128)(2,1)} %all-gather.3.cloned.1.call-done), kind=kLoop, calls=%fused_computation.65 | loop fusion | flops 6290944 | bytes 4196352 | tf_op jit(solution)/shard_map/reduce_sum | solution.py:28
  102.1 45.8 %all-gather.5.cloned.1.call-done = bf16[4096,256]{1,0:T(8,128)(2,1)} async-done(((bf16[256,256]{1,0:T(8,128)(2,1)}), bf16[4096,256]{1,0:T(8,128)(2,1)}) %all-gather.5.cloned.1.call-update) | async-done | bytes 2097168 | tf_op jit(solution)/shard_map/all_gather | solution.py:16
  147.9 3.9 %fusion.53 = bf16[512,1,128]{2,0,1:T(8,128)(2,1)S(1)} fusion(bf16[4096,256]{1,0:T(8,128)(2,1)} %all-gather.5.cloned.1.call-done, bf16[1,512,4096]{2,1,0:T(8,128)(2,1)} %all-gather.3.cloned.1.call-done, f32[4096]{0:T(1024)S(1)} %copy-done.9, f32[512]{0:T(512)S(1)} %add_rsqrt_fusion), kind=kOutput, calls=%fused_computation.73 | convolution fusion | flops 545325056 | bytes 5392384 | tf_op jit(solution)/shard_map/dot_general | solution.py:101
  152.4 1.3 fusion.54
  153.7 8.4 %while.31 = (s32[]{:T(128)}, f32[512,1,128]{0,2,1:T(8,128)}, f32[512,1,128]{0,2,1:T(8,128)S(1)}, bf16[2,512,1,128]{3,1,2,0:T(8,128)(2,1)S(1)}, bf16[2,512,1,128]...) while((s32[]{:T(128)}, f32[512,1,128]{0,2,1:T(8,128)}, ...), condition=%wide.region_10.11_spmd.clone, body=%wide.region_6.10_spmd.clone.sunk | while | flops 340524032 | bytes 11164816 | solution.py:74
  156.1 1.0 fusion.112
  159.8 2.0 fusion.112
  162.2 1.1 convert_bitcast_fusion.2
  163.3 5.2 %convolution_convert_fusion = bf16[4096,256]{1,0:T(8,128)(2,1)} fusion(bf16[512,128]{0,1:T(8,128)(2,1)S(1)} %get-tuple-element.309, bf16[512,128]{0,1:T(8,128)(2,1)S(1)} %get-tuple-element.310, bf16[1,512,4096]{2,1,0:T(8,128)(2,1)} %all-gather.3.cloned.1.call-done, f32[4096]{0:T(1024)S(1)} %copy-done.9, f32[512]{0:T(512)S(1)} %add_rsqrt_fusion), kind=kOutput, calls=%fused_computation.68 | convolution fusion | flops 1083703296 | bytes 6572032 | tf_op jit(solution)/shard_map/dot_general | solution.py:146
  168.6 13.7 %while.30 = (s32[]{:T(128)}, f32[1024,1,128]{0,2,1:T(8,128)S(1)}, f32[1024,1,128]{0,2,1:T(8,128)}, bf16[2,512,1,128]{3,1,2,0:T(8,128)(2,1)S(1)}, bf16[2,512,1,12...) while((s32[]{:T(128)}, f32[1024,1,128]{0,2,1:T(8,128)S(1)}, ...), condition=%wide.region_4.5_spmd.clone, body=%wide.region_0.4_spmd.clone.sunk | while | flops 685243904 | bytes 23622340 | solution.py:74
  170.4 2.6 %fusion.102 = f32[1024,1,128]{0,2,1:T(8,128)} fusion(f32[1024,1,128]{0,2,1:T(8,128)} %get-tuple-element.483, pred[]{:T(512)S(6)} %compare.6, bf16[2,512,1,128]{3,1,2,0:T(8,128)(2,1)} %get-tuple-element.499, s32[]{:T(128)} %get-tuple-element.481, f32[512,1024]{1,0:T(8,128)S(1)} %get-tuple-element.420, f32[512]{0:T(512)S(1)} %fusion.100, ...), kind=kOutput, calls=%fused_computation.10.clone.1 | convolution fusion | flops 137101312 | bytes 3282433 | tf_op jit(solution)/shard_map/while/body/eval_jaxpr/hqk,qhd->khd/dot_general | solution.py:54
  177.1 2.8 %fusion.102 = f32[1024,1,128]{0,2,1:T(8,128)} fusion(f32[1024,1,128]{0,2,1:T(8,128)} %get-tuple-element.483, pred[]{:T(512)S(6)} %compare.6, bf16[2,512,1,128]{3,1,2,0:T(8,128)(2,1)} %get-tuple-element.499, s32[]{:T(128)} %get-tuple-element.481, f32[512,1024]{1,0:T(8,128)S(1)} %get-tuple-element.420, f32[512]{0:T(512)S(1)} %fusion.100, ...), kind=kOutput, calls=%fused_computation.10.clone.1 | convolution fusion | flops 137101312 | bytes 3282433 | tf_op jit(solution)/shard_map/while/body/eval_jaxpr/hqk,qhd->khd/dot_general | solution.py:54
  182.3 1.2 copy.73
  183.7 1.1 pad_maximum_fusion
  184.8 0.8 copy.77
  185.6 34.7 %all_to_all.30 = bf16[4,1024,1,128]{3,0,2,1:T(4,128)(2,1)S(1)} all-to-all(bf16[4,1024,1,128]{3,0,2,1:T(4,128)(2,1)S(1)} %copy.77), channel_id=1, replica_groups=mesh['section'=4,'seq'=8,'dp'=16] {'seq'}, dimensions={1} | all-to-all | bytes 2097152 | tf_op jit(solution)/shard_map/all_to_all | solution.py:22
  220.5 0.9 copy.79
  221.4 0.9 copy.80
  222.3 0.9 copy.81
  223.2 0.9 copy.82
  224.0 6.9 %reduce-scatter.2.cloned.1.call-done = bf16[256,256]{1,0:T(8,128)(2,1)} async-done(((bf16[4096,256]{1,0:T(8,128)(2,1)}), bf16[256,256]{1,0:T(8,128)(2,1)}) %reduce-scatter.2.cloned.1.call-update) | async-done | bytes 131088 | tf_op jit(solution)/shard_map/reduce_scatter | solution.py:145
  230.9 1.6 fusion.66
  (78 shorter events, 18.7 us)
Async XLA Ops:
  7.2 5.8 %copy-start.3 = (bf16[1,128,8,128]{3,2,1,0:T(8,128)(2,1)S(1)}, bf16[1,128,8,128]{3,2,1,0:T(8,128)(2,1)}, u32[]{:S(2)}) copy-start(bf16[1,128,8,128]{3,2,1,0:T(8,128)(2,1)} %param.18) | copy-start | bytes 786436
  7.2 6.6 %copy-start.4 = (bf16[1,128,8,128]{3,2,1,0:T(8,128)(2,1)S(1)}, bf16[1,128,8,128]{3,2,1,0:T(8,128)(2,1)}, u32[]{:S(2)}) copy-start(bf16[1,128,8,128]{3,2,1,0:T(8,128)(2,1)} %param.19) | copy-start | bytes 786436
  7.2 7.3 %copy-start.5 = (bf16[1,128,8,128]{3,2,1,0:T(8,128)(2,1)S(1)}, bf16[1,128,8,128]{3,2,1,0:T(8,128)(2,1)}, u32[]{:S(2)}) copy-start(bf16[1,128,8,128]{3,2,1,0:T(8,128)(2,1)} %param.20) | copy-start | bytes 786436
  7.2 8.1 %copy-start.6 = (bf16[1,128,8,128]{3,2,1,0:T(8,128)(2,1)S(1)}, bf16[1,128,8,128]{3,2,1,0:T(8,128)(2,1)}, u32[]{:S(2)}) copy-start(bf16[1,128,8,128]{3,2,1,0:T(8,128)(2,1)} %param.21) | copy-start | bytes 786436
  7.2 91.8 %all-gather.3.cloned.1.call-start = ((), (), s32[]{:S(2)}) async-start(), calls=%async_computation.3 | async-start | bytes 4718592 | tf_op jit(solution)/shard_map/all_gather | solution.py:96
  7.9 140.0 %all-gather.5.cloned.1.call-start = ((), (), s32[]{:S(2)}) async-start(), calls=%async_computation.4 | async-start | bytes 2228224 | tf_op jit(solution)/shard_map/all_gather | solution.py:16
  14.5 9.1 %copy-start.10 = (s32[16]{0:T(128)S(1)}, s32[16]{0:T(128)}, u32[]{:S(2)}) copy-start(s32[16]{0:T(128)} %param.26) | copy-start | bytes 196
  14.5 9.8 %copy-start.11 = (s32[16]{0:T(128)S(1)}, s32[16]{0:T(128)}, u32[]{:S(2)}) copy-start(s32[16]{0:T(128)} %param.27) | copy-start | bytes 196
  16.1 60.0 %all-to-all-start = ((bf16[6,128,8,128]{3,1,0,2:T(8,128)(2,1)}), bf16[6,128,8,128]{3,1,0,2:T(8,128)(2,1)S(1)}, u32[]{:S(2)}, u32[]{:S(2)}) async-start(bf16[6,128,8,128]{3,1,0,2:T(8,128)(2,1)} %copy_dynamic-update-slice_fusion), calls=%async_computation | async-start | bytes 3145728 | tf_op jit(solution)/shard_map/all_to_all | solution.py:22
  23.6 207.3 %reduce-scatter.2.cloned.1.call-start = ((), (), s32[]{:S(2)}) async-start(), calls=%async_computation.5 | async-start | bytes 2228224 | tf_op jit(solution)/shard_map/reduce_scatter | solution.py:145
  78.0 70.0 %copy-start.9 = (f32[4096]{0:T(1024)S(1)}, f32[4096]{0:T(1024)}, u32[]{:S(2)}) copy-start(f32[4096]{0:T(1024)} %param.23) | copy-start | bytes 49156
  147.9 4.0 %copy-start = (bf16[1,512,4096]{2,1,0:T(8,128)(2,1)S(1)}, bf16[1,512,4096]{2,1,0:T(8,128)(2,1)}, u32[]{:S(2)}) copy-start(bf16[1,512,4096]{2,1,0:T(8,128)(2,1)} %all-gather.3.cloned.1.call-done) | copy-start | bytes 12582916
  147.9 4.4 %copy-start.8 = (bf16[4096,256]{1,0:T(8,128)(2,1)S(1)}, bf16[4096,256]{1,0:T(8,128)(2,1)}, u32[]{:S(2)}) copy-start(bf16[4096,256]{1,0:T(8,128)(2,1)} %all-gather.5.cloned.1.call-done) | copy-start | bytes 6291460
  162.2 6.3 %copy-start.1 = (bf16[2,512,1,128]{3,1,2,0:T(8,128)(2,1)}, bf16[2,512,1,128]{3,1,2,0:T(8,128)(2,1)S(1)}, u32[]{:S(2)}) copy-start(bf16[2,512,1,128]{3,1,2,0:T(8,128)(2,1)S(1)} %get-tuple-element.107) | copy-start | bytes 786436
  170.3 2.6 %copy-start.2 = (bf16[1024,1,128]{2,0,1:T(8,128)(2,1)S(1)}, bf16[1024,1,128]{2,0,1:T(8,128)(2,1)}, u32[]{:S(2)}) copy-start(bf16[1024,1,128]{2,0,1:T(8,128)(2,1)} %get-tuple-element.500) | copy-start | bytes 786436 | tf_op jit(solution)/shard_map/while
  170.3 2.6 %copy-start.7 = (bf16[2,512,1,128]{3,1,2,0:T(8,128)(2,1)S(1)}, bf16[2,512,1,128]{3,1,2,0:T(8,128)(2,1)}, u32[]{:S(2)}) copy-start(bf16[2,512,1,128]{3,1,2,0:T(8,128)(2,1)} %get-tuple-element.499) | copy-start | bytes 786436 | tf_op jit(solution)/shard_map/while
  177.1 2.8 %copy-start.2 = (bf16[1024,1,128]{2,0,1:T(8,128)(2,1)S(1)}, bf16[1024,1,128]{2,0,1:T(8,128)(2,1)}, u32[]{:S(2)}) copy-start(bf16[1024,1,128]{2,0,1:T(8,128)(2,1)} %get-tuple-element.500) | copy-start | bytes 786436 | tf_op jit(solution)/shard_map/while
  177.1 2.8 %copy-start.7 = (bf16[2,512,1,128]{3,1,2,0:T(8,128)(2,1)S(1)}, bf16[2,512,1,128]{3,1,2,0:T(8,128)(2,1)}, u32[]{:S(2)}) copy-start(bf16[2,512,1,128]{3,1,2,0:T(8,128)(2,1)} %get-tuple-element.499) | copy-start | bytes 786436 | tf_op jit(solution)/shard_map/while
Sparse Core Ops, SparseCore 0:
  10.1 88.8 all-gather.2
  101.7 46.1 all-gather.4
  168.7 62.2 reduce-scatter.1
where the time goes:
time: 240 us; the launch traced here: 239 us
  waiting for transfers between devices  125 us (52%)
  blocking collectives  34.7 us (14%)
  matrix products  26 us (11%)
  local copies, waits for them, and re-layouts  16.8 us (7%)
  other arithmetic  14.5 us (6%)
  between operations  13.9 us (6%)
  starting transfers between devices  7.62 us (3%)
    all_to_all x1, waiting for transfers between devices, side_by_side(): lax.all_to_all(both, axis, split_axis=split_dim, concat_axis=concat_dim,...  50.6 us
    all_gather x1, waiting for transfers between devices, sent_together(): lax.all_gather(both, axis, axis=dim, tiled=True)  45.8 us
    all_to_all x1, blocking collectives, side_by_side(): lax.all_to_all(both, axis, split_axis=split_dim, concat_axis=concat_dim,...  34.7 us
    all_gather x1, waiting for transfers between devices, local(): lax.all_gather(caption_states, 'seq', axis=1, tiled=True)  21 us
    unnamed x29, local copies, waits for them, and re-layouts  9.77 us
    all_to_all x1, starting transfers between devices, side_by_side(): lax.all_to_all(both, axis, split_axis=split_dim, concat_axis=concat_dim,...  7.55 us
    reduce_scatter x1, waiting for transfers between devices, local(): lax.psum_scatter(lax.dot_general(columns, stacked, contract_rows, preferr...  6.91 us
    dot_general x4, matrix products, block_gradients(): jnp.einsum('hqk,qhd->khd', weights_low, cotangent_rows, preferred_element...  6.08 us
  transfers between devices with their start and end apart: 4, of which 4 were waited for; matrix products, arithmetic and copies ran while one was open for 15% of the time, Pallas kernels for 0%

commit v1 on v0

--- a/solution.py
+++ b/solution.py
@@ -93,7 +93,12 @@
     score_scale = 1.0 / math.sqrt(head_size)
     head_width = key_weight.shape[1]
     local_heads = head_width // head_size
-    normed = normalize_rows(lax.all_gather(caption_states, "seq", axis=1, tiled=True), caption_gain)
+    normed = normalize_rows(
+        jnp.concatenate(
+            lax.all_to_all(jnp.stack([caption_states] * lax.axis_size("seq")), "seq", 0, 0), axis=1
+        ),
+        caption_gain,
+    )
     normed_text = normed[0]
     caption_rows = normed_text.shape[0]
     pieces = sent_together((key_weight, value_weight), "dp", 0, 1)

time: 240 us -> 262 us (1.092)
  the two profiles are of different devices: /device:TPU:12 before, /device:TPU:10 now
where the time goes in v1:
time: 262 us; the launch traced here: 261 us
  waiting for transfers between devices  101 us (39%)
  blocking collectives  77.5 us (30%)
  matrix products  25 us (10%)
  other arithmetic  18.5 us (7%)
  local copies, waits for them, and re-layouts  17.7 us (7%)
  between operations  14.3 us (5%)
  starting transfers between devices  6.08 us (2%)
    all_to_all x1, waiting for transfers between devices, local(): lax.all_to_all(jnp.stack([caption_states] * lax.axis_size('seq')), 'seq',...  88.8 us
    all_to_all x2, blocking collectives, side_by_side(): lax.all_to_all(both, axis, split_axis=split_dim, concat_axis=concat_dim,...  77.5 us
    reduce_scatter x1, waiting for transfers between devices, local(): lax.psum_scatter(lax.dot_general(columns, stacked, contract_rows, preferr...  12.4 us
    unnamed x29, local copies, waits for them, and re-layouts  7.71 us
    all_to_all x1, starting transfers between devices, local(): lax.all_to_all(jnp.stack([caption_states] * lax.axis_size('seq')), 'seq',...  6.04 us
    dot_general x4, matrix products, block_gradients(): jnp.einsum('hqk,qhd->khd', weights_low, cotangent_rows, preferred_element...  6.01 us
    convert_element_type x1, other arithmetic, normalize_rows(): (values * lax.rsqrt(mean_square + norm_epsilon) * caption_gain).astype(jn...  5.81 us
  transfers between devices with their start and end apart: 3, of which 2 were waited for; matrix products, arithmetic and copies ran while one was open for 13% of the time, Pallas kernels for 0%

profile of v1, /device:TPU:10, one launch (start us, length us, event | category | flops | bytes accessed | tf_op | source)
XLA Modules:
  0.0 260.8 jit_solution(1093272946186726352)
XLA Ops:
  7.2 1.0 copy_dynamic-update-slice_fusion.5
  8.2 1.0 copy_dynamic-update-slice_fusion.4
  9.3 1.0 copy_dynamic-update-slice_fusion.3
  10.3 1.0 copy_dynamic-update-slice_fusion.2
  11.5 45.9 %all_to_all.35 = bf16[6,128,8,128]{3,1,0,2:T(8,128)(2,1)S(1)} all-to-all(bf16[6,128,8,128]{3,1,0,2:T(8,128)(2,1)S(1)} %copy_dynamic-update-slice_fusion), channel_id=1, replica_groups=mesh['section'=4,'seq'=8,'dp'=16] {'seq'}, dimensions={2} | all-to-all | bytes 3145728 | tf_op jit(solution)/shard_map/all_to_all | solution.py:22
  57.3 2.5 stack.2
  59.8 6.0 %all-to-all-start.1 = ((bf16[8,1,64,4096]{3,2,1,0:T(8,128)(2,1)}), bf16[8,1,64,4096]{3,2,1,0:T(8,128)(2,1)}, u32[]{:S(2)}, u32[]{:S(2)}) async-start(bf16[8,1,64,4096]{3,2,1,0:T(8,128)(2,1)} %stack.2), calls=%async_computation.1 | async-start | bytes 8388608 | tf_op jit(solution)/shard_map/all_to_all | solution.py:98
  68.7 0.9 fusion.60
  69.6 0.9 select_bitcast_fusion.1
  70.5 88.8 %all-to-all-done.1 = bf16[8,1,64,4096]{3,2,1,0:T(8,128)(2,1)} async-done(((bf16[8,1,64,4096]{3,2,1,0:T(8,128)(2,1)}), bf16[8,1,64,4096]{3,2,1,0:T(8,128)(2,1)}, u32[]{:S(2)}, u32[]{:S(2)}) %all-to-all-start.1) | async-done | bytes 4194336 | tf_op jit(solution)/shard_map/all_to_all | solution.py:98
  159.3 3.1 %multiply_reduce_fusion.2 = f32[8,64]{1,0:T(8,128)S(1)} fusion(bf16[8,1,64,4096]{3,2,1,0:T(8,128)(2,1)} %all-to-all-done.1), kind=kLoop, calls=%fused_computation.66 | loop fusion | flops 6290944 | bytes 4196352 | tf_op jit(solution)/shard_map/reduce_sum | solution.py:28
  162.5 5.8 %fusion.50 = bf16[512,4096]{1,0:T(8,128)(2,1)} fusion(f32[4096]{0:T(1024)S(1)} %copy-done.9, f32[512]{0:T(512)S(1)} %rsqrt.12, bf16[8,1,64,4096]{3,2,1,0:T(8,128)(2,1)} %all-to-all-done.1), kind=kLoop, calls=%fused_computation.65 | loop fusion | flops 8388608 | bytes 8407040 | tf_op jit(solution)/shard_map/convert_element_type | solution.py:29
  168.3 3.9 %fusion.51 = bf16[512,1,128]{2,0,1:T(8,128)(2,1)S(1)} fusion(bf16[512,4096]{1,0:T(8,128)(2,1)} %fusion.50, bf16[4096,256]{1,0:T(8,128)(2,1)} %all-gather.2.cloned.1.call-done), kind=kOutput, calls=%fused_computation.71 | convolution fusion | flops 536936448 | bytes 5373952 | tf_op jit(solution)/shard_map/dot_general | solution.py:106
  172.2 3.1 %fusion.52 = bf16[512,1,128]{2,0,1:T(8,128)(2,1)} fusion(bf16[512,4096]{1,0:T(8,128)(2,1)S(1)} %copy-done, bf16[4096,256]{1,0:T(8,128)(2,1)} %all-gather.2.cloned.1.call-done), kind=kOutput, calls=%fused_computation.72 | convolution fusion | flops 536936448 | bytes 5373952 | tf_op jit(solution)/shard_map/dot_general | solution.py:107
  175.4 7.1 %while.31 = (s32[]{:T(128)}, f32[512,1,128]{0,2,1:T(8,128)S(1)}, f32[512,1,128]{0,2,1:T(8,128)S(1)}, bf16[2,512,1,128]{3,1,2,0:T(8,128)(2,1)S(1)}, bf16[2,512,1,...) while((s32[]{:T(128)}, f32[512,1,128]{0,2,1:T(8,128)S(1)}, ...), condition=%wide.region_10.11_spmd.clone, body=%wide.region_6.10_spmd.clone.sunk | while | flops 340524032 | bytes 11689132 | solution.py:74
  182.6 4.9 %convolution_convert_fusion = bf16[4096,256]{1,0:T(8,128)(2,1)} fusion(bf16[512,4096]{1,0:T(8,128)(2,1)} %fusion.50, bf16[512,128]{0,1:T(8,128)(2,1)S(1)} %get-tuple-element.333, bf16[512,128]{0,1:T(8,128)(2,1)S(1)} %get-tuple-element.334), kind=kOutput, calls=%fused_computation.67 | convolution fusion | flops 1075314688 | bytes 6553600 | tf_op jit(solution)/shard_map/dot_general | solution.py:151
  187.6 13.7 %while.30 = (s32[]{:T(128)}, f32[1024,1,128]{0,2,1:T(8,128)S(1)}, f32[1024,1,128]{0,2,1:T(8,128)}, bf16[2,512,1,128]{3,1,2,0:T(8,128)(2,1)S(1)}, bf16[2,512,1,12...) while((s32[]{:T(128)}, f32[1024,1,128]{0,2,1:T(8,128)S(1)}, ...), condition=%wide.region_4.5_spmd.clone, body=%wide.region_0.4_spmd.clone.sunk | while | flops 685243904 | bytes 23622340 | solution.py:74
  189.4 2.5 fusion.100
  191.9 0.8 multiply_reduce_fusion.5
  196.1 2.7 %fusion.100 = f32[1024,1,128]{0,2,1:T(8,128)} fusion(f32[1024,1,128]{0,2,1:T(8,128)} %get-tuple-element.507, pred[]{:T(512)S(6)} %compare.6, bf16[2,512,1,128]{3,1,2,0:T(8,128)(2,1)} %get-tuple-element.523, s32[]{:T(128)} %get-tuple-element.505, f32[512,1024]{1,0:T(8,128)S(1)} %get-tuple-element.444, f32[512]{0:T(512)S(1)} %fusion.98, ...), kind=kOutput, calls=%fused_computation.10.clone.1 | convolution fusion | flops 137101312 | bytes 3282433 | tf_op jit(solution)/shard_map/while/body/eval_jaxpr/hqk,qhd->khd/dot_general | solution.py:54
  198.8 0.8 multiply_reduce_fusion.5
  199.6 0.8 multiply_convert_fusion.4
  201.3 1.2 copy.94
  202.7 1.1 pad_maximum_fusion
  203.7 0.8 copy.98
  204.6 31.7 %all_to_all.36 = bf16[4,1024,1,128]{3,0,2,1:T(4,128)(2,1)S(1)} all-to-all(bf16[4,1024,1,128]{3,0,2,1:T(4,128)(2,1)S(1)} %copy.98), channel_id=1, replica_groups=mesh['section'=4,'seq'=8,'dp'=16] {'seq'}, dimensions={1} | all-to-all | bytes 2097152 | tf_op jit(solution)/shard_map/all_to_all | solution.py:22
  236.5 0.9 copy.100
  237.3 0.9 copy.101
  238.2 0.9 copy.102
  239.1 0.9 copy.103
  240.0 12.4 %reduce-scatter.2.cloned.1.call-done = bf16[256,256]{1,0:T(8,128)(2,1)} async-done(((bf16[4096,256]{1,0:T(8,128)(2,1)}), bf16[256,256]{1,0:T(8,128)(2,1)}) %reduce-scatter.2.cloned.1.call-update) | async-done | bytes 131088 | tf_op jit(solution)/shard_map/reduce_scatter | solution.py:150
  252.4 1.6 fusion.61
  (83 shorter events, 16.4 us)
Async XLA Ops:
  7.2 4.1 %copy-start.4 = (bf16[1,128,8,128]{3,2,1,0:T(8,128)(2,1)S(1)}, bf16[1,128,8,128]{3,2,1,0:T(8,128)(2,1)}, u32[]{:S(2)}) copy-start(bf16[1,128,8,128]{3,2,1,0:T(8,128)(2,1)} %param.20) | copy-start | bytes 786436
  7.2 4.2 %copy-start.5 = (bf16[1,128,8,128]{3,2,1,0:T(8,128)(2,1)S(1)}, bf16[1,128,8,128]{3,2,1,0:T(8,128)(2,1)}, u32[]{:S(2)}) copy-start(bf16[1,128,8,128]{3,2,1,0:T(8,128)(2,1)} %param.21) | copy-start | bytes 786436
  11.3 46.0 %copy-start.2 = (bf16[1,64,4096]{2,1,0:T(8,128)(2,1)S(1)}, bf16[1,64,4096]{2,1,0:T(8,128)(2,1)}, u32[]{:S(2)}) copy-start(bf16[1,64,4096]{2,1,0:T(8,128)(2,1)} %param.22) | copy-start | bytes 1572868
  59.8 6.1 %copy-start.7 = (bf16[256,128]{1,0:T(8,128)(2,1)S(1)}, bf16[256,128]{1,0:T(8,128)(2,1)}, u32[]{:S(2)}) copy-start(bf16[256,128]{1,0:T(8,128)(2,1)} %param.25) | copy-start | bytes 196612
  59.8 6.1 %copy-start.8 = (bf16[256,128]{1,0:T(8,128)(2,1)S(1)}, bf16[256,128]{1,0:T(8,128)(2,1)}, u32[]{:S(2)}) copy-start(bf16[256,128]{1,0:T(8,128)(2,1)} %param.24) | copy-start | bytes 196612
  59.8 6.9 %copy-start.10 = (s32[16]{0:T(128)S(1)}, s32[16]{0:T(128)}, u32[]{:S(2)}) copy-start(s32[16]{0:T(128)} %param.26) | copy-start | bytes 196
  59.8 7.5 %copy-start.11 = (s32[16]{0:T(128)S(1)}, s32[16]{0:T(128)}, u32[]{:S(2)}) copy-start(s32[16]{0:T(128)} %param.27) | copy-start | bytes 196
  59.8 99.5 %all-to-all-start.1 = ((bf16[8,1,64,4096]{3,2,1,0:T(8,128)(2,1)}), bf16[8,1,64,4096]{3,2,1,0:T(8,128)(2,1)}, u32[]{:S(2)}, u32[]{:S(2)}) async-start(bf16[8,1,64,4096]{3,2,1,0:T(8,128)(2,1)} %stack.2), calls=%async_computation.1 | async-start | bytes 8388608 | tf_op jit(solution)/shard_map/all_to_all | solution.py:98
  65.9 102.4 %all-gather.2.cloned.1.call-start = ((), (), s32[]{:S(2)}) async-start(), calls=%async_computation.4 | async-start | bytes 2228224 | tf_op jit(solution)/shard_map/all_gather | solution.py:16
  66.6 185.8 %reduce-scatter.2.cloned.1.call-start = ((), (), s32[]{:S(2)}) async-start(), calls=%async_computation.5 | async-start | bytes 2228224 | tf_op jit(solution)/shard_map/reduce_scatter | solution.py:150
  70.5 92.0 %copy-start.9 = (f32[4096]{0:T(1024)S(1)}, f32[4096]{0:T(1024)}, u32[]{:S(2)}) copy-start(f32[4096]{0:T(1024)} %param.23) | copy-start | bytes 49156
  168.3 3.9 %copy-start = (bf16[512,4096]{1,0:T(8,128)(2,1)S(1)}, bf16[512,4096]{1,0:T(8,128)(2,1)}, u32[]{:S(2)}) copy-start(bf16[512,4096]{1,0:T(8,128)(2,1)} %fusion.50) | copy-start | bytes 12582916
  176.8 0.9 copy-start.12
  180.2 0.9 copy-start.12
  182.5 5.0 %copy-start.1 = (bf16[2,512,1,128]{3,1,2,0:T(8,128)(2,1)}, bf16[2,512,1,128]{3,1,2,0:T(8,128)(2,1)S(1)}, u32[]{:S(2)}) copy-start(bf16[2,512,1,128]{3,1,2,0:T(8,128)(2,1)S(1)} %get-tuple-element.107) | copy-start | bytes 786436
  189.3 2.6 copy-start.3
  189.4 2.5 copy-start.6
  196.1 2.7 %copy-start.3 = (bf16[1024,1,128]{2,0,1:T(8,128)(2,1)S(1)}, bf16[1024,1,128]{2,0,1:T(8,128)(2,1)}, u32[]{:S(2)}) copy-start(bf16[1024,1,128]{2,0,1:T(8,128)(2,1)} %get-tuple-element.524) | copy-start | bytes 786436 | tf_op jit(solution)/shard_map/while
  196.1 2.7 %copy-start.6 = (bf16[2,512,1,128]{3,1,2,0:T(8,128)(2,1)S(1)}, bf16[2,512,1,128]{3,1,2,0:T(8,128)(2,1)}, u32[]{:S(2)}) copy-start(bf16[2,512,1,128]{3,1,2,0:T(8,128)(2,1)} %get-tuple-element.523) | copy-start | bytes 786436 | tf_op jit(solution)/shard_map/while
Sparse Core Ops, SparseCore 0:
  69.4 47.0 all-gather.1
  187.6 64.6 reduce-scatter.1
